TPU v7x, 256 devices: a whole 4x4x8 slice. The times are simulated.
256 devices in a mesh: sens: 4 (over y), samp: 64 (over z, x, core).
Axes of the slice: x: 4, y: 4, z: 8, core: 2. Of those that a mesh axis runs over, the one named last changes fastest.
Arguments:
- slopes: bfloat16 [2, 256, 150528], P(None, 'samp', 'sens'), may hold values from -0.0625 to 0.0625
- targets: bfloat16 [2, 16384, 256], P(None, 'samp'), may hold values from -6 to 6
- reconstructor: float32 [4, 64, 32, 128, 128], P('sens', 'samp'), may hold values from -6 to 6
- foot_act: int32 [4, 64, 32], P('sens'), may hold values from 0 to 1, as said below
- foot_slope: int32 [4, 64, 32], P('sens'), may hold values from 0 to 293, as said below
- foot_count: int32 [4, 64], P('sens'), may hold values from 16 to 32, as said below
Outputs:
- fitted: float32 [4, 64, 32, 128, 128], P('sens', 'samp')
- fit_residual: bfloat16 [16384, 256], P('samp')
Inputs may be any that keep to these rules, and one draw needn't show every extreme that they name: `foot_act`: slots 0 to foot_count-1 of a device are live, the rest padding (actuator block 0 and a slope block already named by slot 0); no (actuator block, slope block) pair repeats among live slots; the slope blocks of one actuator block form a run of consecutive blocks modulo 294. `foot_slope`: the live slots of one device name at most 20 distinct slope blocks; for every sens index some device names exactly 20. `foot_count`: for every sens index some device has 32 live slots.
All inputs are finite; a program needn't handle non-finite values.
Results may differ from a plain program's by a relative error of at most 0.0037.
Values may be sent and summed in bfloat16 or wider, within the bound.
A program may use at most 64 MiB of HBM per device.

v0:
```python
import jax
import jax.numpy as jnp
from jax import lax
from jax.sharding import PartitionSpec as P

STEPS = 2


def per_device(slopes, targets, reconstructor, foot_act, foot_slope, foot_count):
    samp_count = lax.axis_size("samp")
    own_index = lax.axis_index("samp")
    block_size = reconstructor.shape[-1]
    slot_count = reconstructor.shape[2]
    groups = slopes.shape[2] // block_size
    samp_dev = slopes.shape[1]
    act_blocks = targets.shape[1] // block_size
    samples = targets.shape[2]
    step_rate = slot_count * block_size / (samples + 3 * slot_count * block_size)
    act_all = foot_act[0]
    slope_all = foot_slope[0]
    count_all = foot_count[0]
    live_all = jnp.arange(slot_count)[None, :] < count_all[:, None]
    own_act = lax.dynamic_index_in_dim(act_all, own_index, 0, keepdims=False)
    own_live = lax.dynamic_index_in_dim(live_all, own_index, 0, keepdims=False)
    act_onehot = ((own_act[None, :] == jnp.arange(act_blocks)[:, None]) & own_live[None, :]).astype(
        jnp.float32
    )
    need_count = slope_all.shape[1]
    weights = reconstructor[0, 0]
    fit_residual = None
    for step in range(STEPS):
        local_rows = slopes[step].reshape(samp_dev, groups, block_size)
        outgoing = jnp.take(local_rows, slope_all.reshape(-1), axis=1)
        outgoing = outgoing.reshape(samp_dev, samp_count, need_count, block_size)
        arrived = lax.all_to_all(outgoing, "samp", split_axis=1, concat_axis=0, tiled=True)
        slot_slopes = arrived.reshape(samples, need_count, block_size)
        weights_low = weights.astype(jnp.bfloat16)
        partial_sums = jnp.einsum(
            "kil,nkl->kin", weights_low, slot_slopes, preferred_element_type=jnp.float32
        )
        summed = jnp.einsum(
            "jk,kin->jin", act_onehot, partial_sums, precision=lax.Precision.HIGHEST
        )
        target_now = targets[step].reshape(act_blocks, block_size, samples)
        total = lax.psum(summed, "sens")
        residual = (total - target_now).astype(jnp.bfloat16)
        slot_residual = jnp.take(residual, own_act, axis=0)
        gradient = jnp.einsum(
            "kin,nkl->kil", slot_residual, slot_slopes, preferred_element_type=jnp.float32
        )
        weights = jnp.where(own_live[:, None, None], weights - step_rate * gradient, weights)
        fit_residual = residual
    return (weights[None, None], fit_residual.reshape(act_blocks * block_size, samples))


def solution(mesh):
    return jax.shard_map(
        per_device,
        mesh=mesh,
        in_specs=(
            P(None, "samp", "sens"),
            P(None, "samp", None),
            P("sens", "samp", None, None, None),
            P("sens", None, None),
            P("sens", None, None),
            P("sens", None),
        ),
        out_specs=(P("sens", "samp", None, None, None), P("samp", None)),
        check_vma=False,
    )
```

profile of v0, /device:TPU:2, one launch (start us, length us, event | category | flops | bytes accessed | tf_op | source)
XLA Modules:
  0.0 260.0 jit_solution(15203739831678689904)
XLA Ops:
  7.2 0.8 copy.50
  8.1 1.3 slice_bitcast_fusion
  9.4 14.6 %gather_fusion.2 = bf16[2048,4,128]{2,1,0:T(4,128)(2,1)} fusion(bf16[4,294,128]{2,0,1:T(4,128)(2,1)S(1)} %get-tuple-element.4, s32[2048]{0:T(1024)S(1)} %fusion.19), kind=kCustom, calls=%fused_computation.2.clone | custom fusion | bytes 4202496 | tf_op jit(solution)/shard_map/jit(_take)/gather | solution.py:33
  24.0 14.5 %gather_fusion = bf16[2048,4,128]{2,1,0:T(4,128)(2,1)} fusion(bf16[4,294,128]{2,0,1:T(4,128)(2,1)S(1)} %get-tuple-element.5, s32[2048]{0:T(1024)S(1)} %fusion.19), kind=kCustom, calls=%fused_computation.clone | custom fusion | bytes 4202496 | tf_op jit(solution)/shard_map/jit(_take)/gather | solution.py:33
  38.4 10.6 %broadcast_select_fusion = (bf16[2048,4,128]{2,1,0:T(4,128)(2,1)S(1)}, bf16[2048,4,128]{2,1,0:T(4,128)(2,1)S(1)}) fusion(bf16[2048,4,128]{2,1,0:T(4,128)(2,1)} %gather_fusion.2, pred[2048]{0:T(1024)(128)(4,1)S(1)} %compare_and_fusion, bf16[2048,4,128]{2,1,0:T(4,128)(2,1)} %gather_fusion), kind=kLoop, calls=%fused_computation.15 | loop fusion | flops 2097152 | bytes 8390656 | tf_op jit(solution)/shard_map/jit(_take)/select_n | solution.py:33
  49.0 1.9 copy.53
  50.9 12.2 %all-to-all-start = ((bf16[4,64,32,128]{3,2,0,1:T(8,128)(2,1)}), bf16[4,64,32,128]{3,2,0,1:T(8,128)(2,1)}, u32[]{:S(2)}, u32[]{:S(2)}) async-start(bf16[4,64,32,128]{3,2,0,1:T(8,128)(2,1)} %copy.53), calls=%async_computation | async-start | bytes 4194304 | tf_op jit(solution)/shard_map/all_to_all | solution.py:35
  63.1 1.9 copy.59
  65.1 49.2 %all-to-all-done = bf16[4,64,32,128]{3,2,0,1:T(8,128)(2,1)} async-done(((bf16[4,64,32,128]{3,2,0,1:T(8,128)(2,1)}), bf16[4,64,32,128]{3,2,0,1:T(8,128)(2,1)}, u32[]{:S(2)}, u32[]{:S(2)}) %all-to-all-start) | async-done | bytes 2097184 | tf_op jit(solution)/shard_map/all_to_all | solution.py:35
  114.3 5.4 %all-to-all-start.1 = ((bf16[4,64,32,128]{3,2,0,1:T(8,128)(2,1)}), bf16[4,64,32,128]{3,2,0,1:T(8,128)(2,1)S(1)}, u32[]{:S(2)}, u32[]{:S(2)}) async-start(bf16[4,64,32,128]{3,2,0,1:T(8,128)(2,1)} %copy.59), calls=%async_computation.1 | async-start | bytes 4194304 | tf_op jit(solution)/shard_map/all_to_all | solution.py:35
  119.8 0.6 dynamic-slice.1
  120.6 0.7 compare_bitcast_fusion
  121.3 2.8 %copy.54 = bf16[64,4,1,32,128]{4,1,0,3,2:T(4,128)(2,1)S(1)} copy(bf16[64,4,1,32,128]{4,3,1,0,2:T(8,128)(2,1)} %bitcast.8) | data formatting | bytes 4194304 | tf_op jit(solution)/shard_map/all_to_all | solution.py:35
  124.1 1.3 copy-done.2
  125.4 2.7 %convolution_bitcast_fusion = f32[32,128,256]{1,2,0:T(8,128)} fusion(bf16[256,32,128]{2,0,1:T(8,128)(2,1)S(1)} %bitcast.54, f32[1,1,32,128,128]{4,3,2,1,0:T(8,128)S(1)} %copy-done.4), kind=kOutput, calls=%fused_computation.8 | convolution fusion | flops 268435456 | bytes 8388608 | tf_op jit(solution)/shard_map/kil,nkl->kin/dot_general | solution.py:38
  128.1 5.5 %copy.55 = f32[32,128,256]{2,0,1:T(8,128)} copy(f32[32,128,256]{1,2,0:T(8,128)} %convolution_bitcast_fusion) | data formatting | bytes 8388608 | tf_op jit(solution)/shard_map/kil,nkl->kin/dot_general | solution.py:38
  133.6 3.7 %fusion.21 = f32[2,128,256]{2,0,1:T(2,128)S(1)} fusion(f32[32,128,256]{2,0,1:T(8,128)} %copy.55, pred[32]{0:T(512)(128)(4,1)S(1)} %compare_bitcast_fusion, s32[32]{0:T(128)S(1)} %dynamic-slice_reduce_fusion), kind=kOutput, calls=%fused_computation.36 | convolution fusion | flops 25165952 | bytes 4456608 | tf_op jit(solution)/shard_map/jk,kin->jin/dot_general | solution.py:41
  137.3 0.7 copy.56
  138.0 0.2 all-reduce.5.cloned.1.call-start
  138.3 32.7 %all-to-all-done.1 = bf16[4,64,32,128]{3,2,0,1:T(8,128)(2,1)S(1)} async-done(((bf16[4,64,32,128]{3,2,0,1:T(8,128)(2,1)}), bf16[4,64,32,128]{3,2,0,1:T(8,128)(2,1)S(1)}, u32[]{:S(2)}, u32[]{:S(2)}) %all-to-all-start.1) | async-done | bytes 2097184 | tf_op jit(solution)/shard_map/all_to_all | solution.py:35
  171.0 2.4 copy.60
  173.4 12.8 %all-reduce.3.cloned.1.call-done = f32[2,128,256]{2,1,0:T(8,128)} async-done(((f32[2,128,256]{2,1,0:T(8,128)}), f32[2,128,256]{2,1,0:T(8,128)}) %all-reduce.3.cloned.1.call-update) | async-done | bytes 262160 | tf_op jit(solution)/shard_map/psum | solution.py:45
  186.2 1.0 fusion.18
  187.2 2.0 gather_fusion.1
  189.2 3.8 %subtract_select_fusion.1 = f32[32,128,128]{2,1,0:T(8,128)S(1)} fusion(f32[1,1,32,128,128]{4,3,2,1,0:T(8,128)} %param.12, bf16[256,32,128]{2,0,1:T(8,128)(2,1)} %bitcast.55, bf16[32,128,256]{2,1,0:T(8,128)(2,1)} %gather_fusion.1, pred[32]{0:T(512)(128)(4,1)S(1)} %compare_and_fusion.1, pred[32]{0:T(512)(128)(4,1)S(1)} %compare_bitcast_fusion), kind=kOutput, calls=%fused_computation.7 | convolution fusion | flops 271056896 | bytes 8388672 | tf_op jit(solution)/shard_map/kin,nkl->kil/dot_general | solution.py:48
  193.0 0.7 fusion.15
  193.8 3.8 %fusion = f32[2,128,256]{2,0,1:T(2,128)S(1)} fusion(f32[32,128,256]{2,1,0:T(8,128)S(1)} %fusion.15, pred[32]{0:T(512)(128)(4,1)S(1)} %compare_bitcast_fusion, s32[32]{0:T(128)S(1)} %dynamic-slice_reduce_fusion), kind=kOutput, calls=%fused_computation.4 | convolution fusion | flops 25165952 | bytes 4456608 | tf_op jit(solution)/shard_map/jk,kin->jin/dot_general | solution.py:41
  197.6 0.7 copy.62
  198.3 47.4 %all-reduce.5.cloned.1.call-done = f32[2,128,256]{2,1,0:T(8,128)} async-done(((f32[2,128,256]{2,1,0:T(8,128)}), f32[2,128,256]{2,1,0:T(8,128)}) %all-reduce.5.cloned.1.call-update) | async-done | bytes 262160 | tf_op jit(solution)/shard_map/psum | solution.py:45
  245.8 1.0 fusion.17
  246.7 2.0 gather_fusion.3
  248.8 4.4 %fusion.2 = f32[1,1,32,128,128]{4,3,2,1,0:T(8,128)} fusion(f32[32,128,128]{2,1,0:T(8,128)S(1)} %subtract_select_fusion.1, bf16[256,32,128]{2,0,1:T(8,128)(2,1)} %bitcast.56, bf16[32,128,256]{2,1,0:T(8,128)(2,1)} %gather_fusion.3, pred[32]{0:T(512)(128)(4,1)S(1)} %compare_and_fusion.1, pred[32]{0:T(512)(128)(4,1)S(1)} %compare_bitcast_fusion), kind=kOutput, calls=%fused_computation.9 | convolution fusion | flops 271056896 | bytes 8388672 | tf_op jit(solution)/shard_map/kin,nkl->kil/dot_general | solution.py:48
  (24 shorter events, 0.4 us)
Async XLA Ops:
  7.2 113.3 %copy-start = (s32[1,64,32]{1,2,0:T(8,128)S(1)}, s32[1,64,32]{1,2,0:T(8,128)}, u32[]{:S(2)}) copy-start(s32[1,64,32]{1,2,0:T(8,128)} %param.13) | copy-start | bytes 24580
  50.9 63.4 %all-to-all-start = ((bf16[4,64,32,128]{3,2,0,1:T(8,128)(2,1)}), bf16[4,64,32,128]{3,2,0,1:T(8,128)(2,1)}, u32[]{:S(2)}, u32[]{:S(2)}) async-start(bf16[4,64,32,128]{3,2,0,1:T(8,128)(2,1)} %copy.53), calls=%async_computation | async-start | bytes 4194304 | tf_op jit(solution)/shard_map/all_to_all | solution.py:35
  65.1 54.7 %copy-start.6 = (s32[1,64]{1,0:T(1,128)S(1)}, s32[1,64]{1,0:T(1,128)}, u32[]{:S(2)}) copy-start(s32[1,64]{1,0:T(1,128)} %param.15) | copy-start | bytes 772
  114.3 56.7 %all-to-all-start.1 = ((bf16[4,64,32,128]{3,2,0,1:T(8,128)(2,1)}), bf16[4,64,32,128]{3,2,0,1:T(8,128)(2,1)S(1)}, u32[]{:S(2)}, u32[]{:S(2)}) async-start(bf16[4,64,32,128]{3,2,0,1:T(8,128)(2,1)} %copy.59), calls=%async_computation.1 | async-start | bytes 4194304 | tf_op jit(solution)/shard_map/all_to_all | solution.py:35
  119.8 66.4 %all-reduce.3.cloned.1.call-start = ((), (), s32[]{:S(2)}) async-start(), calls=%async_computation.2 | async-start | bytes 524288 | tf_op jit(solution)/shard_map/psum | solution.py:45
  121.3 4.2 %copy-start.4 = (f32[1,1,32,128,128]{4,3,2,1,0:T(8,128)S(1)}, f32[1,1,32,128,128]{4,3,2,1,0:T(8,128)}, u32[]{:S(2)}) copy-start(f32[1,1,32,128,128]{4,3,2,1,0:T(8,128)} %param.12) | copy-start | bytes 6291460
  124.1 1.3 copy-start.2
  133.6 4.7 %copy-start.5 = (bf16[2,256,256]{2,1,0:T(8,128)(2,1)S(1)}, bf16[2,256,256]{2,1,0:T(8,128)(2,1)}, u32[]{:S(2)}) copy-start(bf16[2,256,256]{2,1,0:T(8,128)(2,1)} %param.11) | copy-start | bytes 786436
  138.0 107.7 %all-reduce.5.cloned.1.call-start = ((), (), s32[]{:S(2)}) async-start(), calls=%async_computation.3 | async-start | bytes 524288 | tf_op jit(solution)/shard_map/psum | solution.py:45
  189.2 3.9 %copy-start.3 = (bf16[64,4,1,32,128]{4,1,0,3,2:T(4,128)(2,1)S(1)}, bf16[64,4,1,32,128]{4,1,0,3,2:T(4,128)(2,1)}, u32[]{:S(2)}) copy-start(bf16[64,4,1,32,128]{4,1,0,3,2:T(4,128)(2,1)} %copy.60) | copy-start | bytes 6291460
  246.7 2.0 copy-start.1
Sparse Core Ops, SparseCore 0:
  138.1 48.0 all-reduce.2
  198.5 47.2 all-reduce.4
where the time goes:
time: 261 us; the launch traced here: 260 us
  waiting for transfers between devices  142 us (54%)
  local copies, waits for them, and re-layouts  53.4 us (20%)
  matrix products  19.1 us (7%)
  starting transfers between devices  17.9 us (7%)
  between operations  14.2 us (5%)
  other arithmetic  13.2 us (5%)
    all_to_all x2, waiting for transfers between devices, per_device(): lax.all_to_all(outgoing, 'samp', split_axis=1, concat_axis=0, tiled=True)  82 us
    psum x2, waiting for transfers between devices, per_device(): total = lax.psum(summed, 'sens')  60.2 us
    gather x2, local copies, waits for them, and re-layouts, per_device(): outgoing = jnp.take(local_rows, slope_all.reshape(-1), axis=1)  29.1 us
    all_to_all x2, starting transfers between devices, per_device(): lax.all_to_all(outgoing, 'samp', split_axis=1, concat_axis=0, tiled=True)  17.6 us
    select_n x1, other arithmetic, per_device(): outgoing = jnp.take(local_rows, slope_all.reshape(-1), axis=1)  10.6 us
    dot_general x2, matrix products, per_device(): jnp.einsum('kin,nkl->kil', slot_residual, slot_slopes, preferred_element_...  8.22 us
    dot_general x2, matrix products, per_device(): jnp.einsum('jk,kin->jin', act_onehot, partial_sums, precision=lax.Precisi...  7.5 us
    dot_general x1, local copies, waits for them, and re-layouts, per_device(): jnp.einsum('kil,nkl->kin', weights_low, slot_slopes, preferred_element_ty...  5.48 us
  transfers between devices with their start and end apart: 4, of which 4 were waited for; matrix products, arithmetic and copies ran while one was open for 8% of the time, Pallas kernels for 0%

commit v1 on v0

--- a/solution.py
+++ b/solution.py
@@ -1,9 +1,17 @@
+import functools
 import jax
 import jax.numpy as jnp
 from jax import lax
 from jax.sharding import PartitionSpec as P
 
 STEPS = 2
+
+
+def expand_run(sample, shard_axis):
+    return lax.all_gather(sample, shard_axis).sum(axis=0)
+
+
+feed_unit = functools.partial(expand_run, shard_axis="sens")
 
 
 def per_device(slopes, targets, reconstructor, foot_act, foot_slope, foot_count):
@@ -42,7 +50,7 @@
             "jk,kin->jin", act_onehot, partial_sums, precision=lax.Precision.HIGHEST
         )
         target_now = targets[step].reshape(act_blocks, block_size, samples)
-        total = lax.psum(summed, "sens")
+        total = feed_unit(summed)
         residual = (total - target_now).astype(jnp.bfloat16)
         slot_residual = jnp.take(residual, own_act, axis=0)
         gradient = jnp.einsum(

time: 261 us -> 225 us (0.86)
  waiting for transfers between devices: 142 us -> 105 us
    psum x2 -> x0, waiting for transfers between devices: 60.2 us -> none  [per_device(): total = lax.psum(summed, 'sens')]
    all_gather x0 -> x2, waiting for transfers between devices: none -> 23.1 us  [expand_run(): return lax.all_gather(sample, shard_axis).sum(axis=0)]
    reduce_sum x0 -> x2, other arithmetic: none -> 2.64 us  [expand_run(): return lax.all_gather(sample, shard_axis).sum(axis=0)]
  transfers between devices with their start and end apart: 4 -> 4, of which waited for: 4 -> 3; matrix products, arithmetic and copies ran while one was open for 8% -> 9% of each run, Pallas kernels for 0% -> 0%
where the time goes in v1:
time: 225 us; the launch traced here: 224 us
  waiting for transfers between devices  105 us (47%)
  local copies, waits for them, and re-layouts  53.4 us (24%)
  matrix products  19.1 us (8%)
  starting transfers between devices  17.9 us (8%)
  other arithmetic  14.7 us (7%)
  between operations  14.2 us (6%)
    all_to_all x2, waiting for transfers between devices, per_device(): lax.all_to_all(outgoing, 'samp', split_axis=1, concat_axis=0, tiled=True)  82 us
    gather x2, local copies, waits for them, and re-layouts, per_device(): outgoing = jnp.take(local_rows, slope_all.reshape(-1), axis=1)  29.2 us
    all_gather x2, waiting for transfers between devices, expand_run(): return lax.all_gather(sample, shard_axis).sum(axis=0)  23.1 us
    all_to_all x2, starting transfers between devices, per_device(): lax.all_to_all(outgoing, 'samp', split_axis=1, concat_axis=0, tiled=True)  17.6 us
    select_n x1, other arithmetic, per_device(): outgoing = jnp.take(local_rows, slope_all.reshape(-1), axis=1)  10.6 us
    dot_general x2, matrix products, per_device(): jnp.einsum('kin,nkl->kil', slot_residual, slot_slopes, preferred_element_...  8.22 us
    dot_general x2, matrix products, per_device(): jnp.einsum('jk,kin->jin', act_onehot, partial_sums, precision=lax.Precisi...  7.5 us
    dot_general x1, local copies, waits for them, and re-layouts, per_device(): jnp.einsum('kil,nkl->kin', weights_low, slot_slopes, preferred_element_ty...  5.48 us
  transfers between devices with their start and end apart: 4, of which 3 were waited for; matrix products, arithmetic and copies ran while one was open for 9% of the time, Pallas kernels for 0%

profile of v1, /device:TPU:2, one launch (start us, length us, event | category | flops | bytes accessed | tf_op | source)
XLA Modules:
  0.0 224.4 jit_solution(10309722219496960412)
XLA Ops:
  7.2 0.8 copy.32
  8.1 1.3 slice_bitcast_fusion
  9.4 14.6 %gather_fusion.2 = bf16[2048,4,128]{2,1,0:T(4,128)(2,1)} fusion(bf16[4,294,128]{2,0,1:T(4,128)(2,1)S(1)} %get-tuple-element.4, s32[2048]{0:T(1024)S(1)} %fusion.19), kind=kCustom, calls=%fused_computation.2.clone | custom fusion | bytes 4202496 | tf_op jit(solution)/shard_map/jit(_take)/gather | solution.py:41
  24.0 14.6 %gather_fusion = bf16[2048,4,128]{2,1,0:T(4,128)(2,1)} fusion(bf16[4,294,128]{2,0,1:T(4,128)(2,1)S(1)} %get-tuple-element.5, s32[2048]{0:T(1024)S(1)} %fusion.19), kind=kCustom, calls=%fused_computation.clone | custom fusion | bytes 4202496 | tf_op jit(solution)/shard_map/jit(_take)/gather | solution.py:41
  38.5 10.6 %broadcast_select_fusion = (bf16[2048,4,128]{2,1,0:T(4,128)(2,1)S(1)}, bf16[2048,4,128]{2,1,0:T(4,128)(2,1)S(1)}) fusion(bf16[2048,4,128]{2,1,0:T(4,128)(2,1)} %gather_fusion.2, pred[2048]{0:T(1024)(128)(4,1)S(1)} %compare_and_fusion, bf16[2048,4,128]{2,1,0:T(4,128)(2,1)} %gather_fusion), kind=kLoop, calls=%fused_computation.15 | loop fusion | flops 2097152 | bytes 8390656 | tf_op jit(solution)/shard_map/jit(_take)/select_n | solution.py:41
  49.1 1.9 copy.35
  51.0 12.2 %all-to-all-start = ((bf16[4,64,32,128]{3,2,0,1:T(8,128)(2,1)}), bf16[4,64,32,128]{3,2,0,1:T(8,128)(2,1)}, u32[]{:S(2)}, u32[]{:S(2)}) async-start(bf16[4,64,32,128]{3,2,0,1:T(8,128)(2,1)} %copy.35), calls=%async_computation | async-start | bytes 4194304 | tf_op jit(solution)/shard_map/all_to_all | solution.py:43
  63.2 1.9 copy.43
  65.2 49.2 %all-to-all-done = bf16[4,64,32,128]{3,2,0,1:T(8,128)(2,1)} async-done(((bf16[4,64,32,128]{3,2,0,1:T(8,128)(2,1)}), bf16[4,64,32,128]{3,2,0,1:T(8,128)(2,1)}, u32[]{:S(2)}, u32[]{:S(2)}) %all-to-all-start) | async-done | bytes 2097184 | tf_op jit(solution)/shard_map/all_to_all | solution.py:43
  114.4 5.4 %all-to-all-start.1 = ((bf16[4,64,32,128]{3,2,0,1:T(8,128)(2,1)}), bf16[4,64,32,128]{3,2,0,1:T(8,128)(2,1)S(1)}, u32[]{:S(2)}, u32[]{:S(2)}) async-start(bf16[4,64,32,128]{3,2,0,1:T(8,128)(2,1)} %copy.43), calls=%async_computation.1 | async-start | bytes 4194304 | tf_op jit(solution)/shard_map/all_to_all | solution.py:43
  119.9 0.6 dynamic-slice.1
  120.7 0.7 compare_bitcast_fusion
  121.4 2.8 %copy.36 = bf16[64,4,1,32,128]{4,1,0,3,2:T(4,128)(2,1)S(1)} copy(bf16[64,4,1,32,128]{4,3,1,0,2:T(8,128)(2,1)} %bitcast.8) | data formatting | bytes 4194304 | tf_op jit(solution)/shard_map/all_to_all | solution.py:43
  124.2 1.3 copy-done.2
  125.5 2.7 %convolution_bitcast_fusion = f32[32,128,256]{1,2,0:T(8,128)} fusion(bf16[256,32,128]{2,0,1:T(8,128)(2,1)S(1)} %bitcast.61, f32[1,1,32,128,128]{4,3,2,1,0:T(8,128)S(1)} %copy-done.3), kind=kOutput, calls=%fused_computation.8 | convolution fusion | flops 268435456 | bytes 8388608 | tf_op jit(solution)/shard_map/kil,nkl->kin/dot_general | solution.py:46
  128.2 5.5 %copy.37 = f32[32,128,256]{2,0,1:T(8,128)} copy(f32[32,128,256]{1,2,0:T(8,128)} %convolution_bitcast_fusion) | data formatting | bytes 8388608 | tf_op jit(solution)/shard_map/kil,nkl->kin/dot_general | solution.py:46
  133.6 3.7 %fusion.21 = f32[2,128,256]{2,0,1:T(2,128)S(1)} fusion(f32[32,128,256]{2,0,1:T(8,128)} %copy.37, pred[32]{0:T(512)(128)(4,1)S(1)} %compare_bitcast_fusion, s32[32]{0:T(128)S(1)} %dynamic-slice_reduce_fusion), kind=kOutput, calls=%fused_computation.38 | convolution fusion | flops 25165952 | bytes 4456608 | tf_op jit(solution)/shard_map/jk,kin->jin/dot_general | solution.py:49
  137.3 0.7 copy.38
  138.1 0.2 all-gather.7.cloned.1.call-start
  138.4 32.7 %all-to-all-done.1 = bf16[4,64,32,128]{3,2,0,1:T(8,128)(2,1)S(1)} async-done(((bf16[4,64,32,128]{3,2,0,1:T(8,128)(2,1)}), bf16[4,64,32,128]{3,2,0,1:T(8,128)(2,1)S(1)}, u32[]{:S(2)}, u32[]{:S(2)}) %all-to-all-start.1) | async-done | bytes 2097184 | tf_op jit(solution)/shard_map/all_to_all | solution.py:43
  171.1 2.4 %copy.44 = bf16[64,4,1,32,128]{4,1,0,3,2:T(4,128)(2,1)} copy(bf16[64,4,1,32,128]{4,3,1,0,2:T(8,128)(2,1)S(1)} %bitcast.65) | data formatting | bytes 4194304 | tf_op jit(solution)/shard_map/all_to_all | solution.py:43
  173.5 1.3 reduce_sum.20
  174.9 2.0 gather_fusion.1
  176.9 3.8 %subtract_select_fusion.1 = f32[32,128,128]{2,1,0:T(8,128)S(1)} fusion(f32[1,1,32,128,128]{4,3,2,1,0:T(8,128)} %param.12, bf16[256,32,128]{2,0,1:T(8,128)(2,1)} %bitcast.62, bf16[32,128,256]{2,1,0:T(8,128)(2,1)} %gather_fusion.1, pred[32]{0:T(512)(128)(4,1)S(1)} %compare_and_fusion.1, pred[32]{0:T(512)(128)(4,1)S(1)} %compare_bitcast_fusion), kind=kOutput, calls=%fused_computation.7 | convolution fusion | flops 271056896 | bytes 8388672 | tf_op jit(solution)/shard_map/kin,nkl->kil/dot_general | solution.py:56
  180.7 0.7 fusion.15
  181.5 3.8 %fusion = f32[2,128,256]{2,0,1:T(2,128)S(1)} fusion(f32[32,128,256]{2,1,0:T(8,128)S(1)} %fusion.15, pred[32]{0:T(512)(128)(4,1)S(1)} %compare_bitcast_fusion, s32[32]{0:T(128)S(1)} %dynamic-slice_reduce_fusion), kind=kOutput, calls=%fused_computation.4 | convolution fusion | flops 25165952 | bytes 4456608 | tf_op jit(solution)/shard_map/jk,kin->jin/dot_general | solution.py:49
  185.3 0.7 copy.46
  186.0 23.1 %all-gather.7.cloned.1.call-done = f32[8,128,256]{2,1,0:T(8,128)} async-done(((f32[2,128,256]{2,1,0:T(8,128)}), f32[8,128,256]{2,1,0:T(8,128)}) %all-gather.7.cloned.1.call-update) | async-done | bytes 1048592 | tf_op jit(solution)/shard_map/all_gather | solution.py:11
  209.1 1.3 reduce_sum.21
  210.4 0.7 fusion.18
  211.1 2.0 gather_fusion.3
  213.2 4.4 %fusion.2 = f32[1,1,32,128,128]{4,3,2,1,0:T(8,128)} fusion(f32[32,128,128]{2,1,0:T(8,128)S(1)} %subtract_select_fusion.1, bf16[256,32,128]{2,0,1:T(8,128)(2,1)} %bitcast.59, bf16[32,128,256]{2,1,0:T(8,128)(2,1)} %gather_fusion.3, pred[32]{0:T(512)(128)(4,1)S(1)} %compare_and_fusion.1, pred[32]{0:T(512)(128)(4,1)S(1)} %compare_bitcast_fusion), kind=kOutput, calls=%fused_computation.9 | convolution fusion | flops 271056896 | bytes 8388672 | tf_op jit(solution)/shard_map/kin,nkl->kil/dot_general | solution.py:56
  (25 shorter events, 0.5 us)
Async XLA Ops:
  7.2 113.3 %copy-start = (s32[1,64,32]{1,2,0:T(8,128)S(1)}, s32[1,64,32]{1,2,0:T(8,128)}, u32[]{:S(2)}) copy-start(s32[1,64,32]{1,2,0:T(8,128)} %param.13) | copy-start | bytes 24580
  51.0 63.4 %all-to-all-start = ((bf16[4,64,32,128]{3,2,0,1:T(8,128)(2,1)}), bf16[4,64,32,128]{3,2,0,1:T(8,128)(2,1)}, u32[]{:S(2)}, u32[]{:S(2)}) async-start(bf16[4,64,32,128]{3,2,0,1:T(8,128)(2,1)} %copy.35), calls=%async_computation | async-start | bytes 4194304 | tf_op jit(solution)/shard_map/all_to_all | solution.py:43
  65.2 54.7 %copy-start.5 = (s32[1,64]{1,0:T(1,128)S(1)}, s32[1,64]{1,0:T(1,128)}, u32[]{:S(2)}) copy-start(s32[1,64]{1,0:T(1,128)} %param.15) | copy-start | bytes 772
  114.4 56.7 %all-to-all-start.1 = ((bf16[4,64,32,128]{3,2,0,1:T(8,128)(2,1)}), bf16[4,64,32,128]{3,2,0,1:T(8,128)(2,1)S(1)}, u32[]{:S(2)}, u32[]{:S(2)}) async-start(bf16[4,64,32,128]{3,2,0,1:T(8,128)(2,1)} %copy.43), calls=%async_computation.1 | async-start | bytes 4194304 | tf_op jit(solution)/shard_map/all_to_all | solution.py:43
  119.8 53.7 %all-gather.5.cloned.1.call-start = ((), (), s32[]{:S(2)}) async-start(), calls=%async_computation.2 | async-start | bytes 1310720 | tf_op jit(solution)/shard_map/all_gather | solution.py:11
  121.3 4.2 %copy-start.3 = (f32[1,1,32,128,128]{4,3,2,1,0:T(8,128)S(1)}, f32[1,1,32,128,128]{4,3,2,1,0:T(8,128)}, u32[]{:S(2)}) copy-start(f32[1,1,32,128,128]{4,3,2,1,0:T(8,128)} %param.12) | copy-start | bytes 6291460
  124.2 1.3 copy-start.2
  133.6 4.7 %copy-start.4 = (bf16[2,256,256]{2,1,0:T(8,128)(2,1)S(1)}, bf16[2,256,256]{2,1,0:T(8,128)(2,1)}, u32[]{:S(2)}) copy-start(bf16[2,256,256]{2,1,0:T(8,128)(2,1)} %param.11) | copy-start | bytes 786436
  138.1 71.0 %all-gather.7.cloned.1.call-start = ((), (), s32[]{:S(2)}) async-start(), calls=%async_computation.3 | async-start | bytes 1310720 | tf_op jit(solution)/shard_map/all_gather | solution.py:11
  176.9 3.8 %copy-start.1 = (bf16[64,4,1,32,128]{4,1,0,3,2:T(4,128)(2,1)S(1)}, bf16[64,4,1,32,128]{4,1,0,3,2:T(4,128)(2,1)}, u32[]{:S(2)}) copy-start(bf16[64,4,1,32,128]{4,1,0,3,2:T(4,128)(2,1)} %copy.44) | copy-start | bytes 6291460
Sparse Core Ops, SparseCore 0:
  138.2 27.7 all-gather.4
  186.2 22.9 all-gather.6
